TPU v7x, 512 devices: a whole 4x8x8 slice. The times are simulated.
512 devices in a mesh: head: 8 (over x, core), blk: 64 (over y, z).
Axes of the slice: x: 4, y: 8, z: 8, core: 2. Of those that a mesh axis runs over, the one named last changes fastest.
Arguments:
- suffix_hidden: bfloat16 [1536, 2048], P('blk'), may hold values from -400 to 400
- prefix_hidden: bfloat16 [16384, 2048], P('blk'), may hold values from -400 to 400
- kv_cache: bfloat16 [2, 16384, 8, 256], P(None, 'blk', 'head'), may hold values from -300 to 300
- norm_gain: float32 [2048], replicated, may hold values from 0.1 to 1.9
- norm_bias: float32 [2048], replicated, may hold values from -3 to 3
- qkv_weight: bfloat16 [2048, 8, 768], P('blk', 'head'), may hold values from -0.125 to 0.125
- qkv_bias: float32 [8, 768], P('head'), may hold values from -3 to 3
- out_weight: bfloat16 [8, 256, 2048], P('head', 'blk'), may hold values from -0.125 to 0.125
- out_bias: float32 [2048], replicated, may hold values from -3 to 3
- suffix_lengths: int32 [4], replicated, may hold values from 1 to 768, 1536 in all
- prefix_blocks: int32 [4], replicated, may hold values from 1 to 32, 64 in all
- block_owner: int32 [64], replicated, may hold values from 0 to 63, each once
- recompute_flag: int32 [16384], P('blk'), may hold values from 0 to 1, as said below
Outputs:
- attn_out: bfloat16 [1536, 2048], P('blk', 'head')
Inputs may be any that keep to these rules, and one draw needn't show every extreme that they name: `recompute_flag`: each storage block of 256 cache rows holds exactly 25 ones.
All inputs are finite; a program needn't handle non-finite values.
Results may differ from a plain program's by a relative error of at most 0.015.
Values may be sent and summed in bfloat16 or wider, within the bound.
A program may use at most 64 MiB of HBM per device.

v0:
```python
import math
import jax
import jax.numpy as jnp
from jax import lax
from jax.sharding import PartitionSpec as P

FLAG_DEV = 25
EPSILON = 1e-05
MASKED = -1e30


def layer_norm(states, norm_scale, norm_shift):
    widened = states.astype(jnp.float32)
    average = jnp.mean(widened, axis=-1, keepdims=True)
    center = widened - average
    variance = jnp.mean(center * center, axis=-1, keepdims=True)
    return (center * lax.rsqrt(variance + EPSILON) * norm_scale + norm_shift).astype(jnp.bfloat16)


def body(
    suffix_hidden,
    prefix_hidden,
    kv_cache,
    norm_gain,
    norm_bias,
    qkv_weight,
    qkv_bias,
    out_weight,
    out_bias,
    suffix_lengths,
    prefix_blocks,
    block_owner,
    recompute_flag,
):
    blk_total = lax.axis_size("blk")
    own_index = lax.axis_index("blk")
    row_count = suffix_hidden.shape[0]
    cache_rows = prefix_hidden.shape[0]
    heads_dev = qkv_weight.shape[1]
    head_dim = qkv_weight.shape[2] // 3
    total_rows = row_count * blk_total
    own_first = own_index * row_count
    tenant_ends = jnp.cumsum(suffix_lengths)
    row_ids = jnp.arange(total_rows, dtype=jnp.int32)
    row_tenant = jnp.sum((row_ids[:, None] >= tenant_ends[None, :]).astype(jnp.int32), axis=1)
    block_ends = jnp.cumsum(prefix_blocks)
    block_slots = jnp.arange(blk_total, dtype=jnp.int32)
    global_block = jnp.sum(jnp.where(block_owner == own_index, block_slots, 0))
    block_tenant = jnp.sum((global_block >= block_ends).astype(jnp.int32))
    normed = layer_norm(suffix_hidden, norm_gain, norm_bias)
    flagged = jnp.argsort(1 - recompute_flag, stable=True)[:FLAG_DEV]
    prefix_normed = layer_norm(prefix_hidden[flagged], norm_gain, norm_bias)
    fetched = lax.all_gather(qkv_weight, "blk", axis=0, tiled=True)
    piece_rows = fetched.shape[0]
    flattened = fetched.reshape(piece_rows, heads_dev * 3 * head_dim)
    kv_part = fetched[:, :, head_dim:].reshape(piece_rows, heads_dev * 2 * head_dim)
    suffix_acc = jnp.dot(normed, flattened, preferred_element_type=jnp.float32)
    prefix_acc = jnp.dot(prefix_normed, kv_part, preferred_element_type=jnp.float32)
    suffix_acc, prefix_acc = (suffix_acc, prefix_acc)
    projected = (
        (suffix_acc + qkv_bias.reshape(-1))
        .astype(jnp.bfloat16)
        .reshape(row_count, heads_dev, 3 * head_dim)
    )
    recomputed = (
        (prefix_acc + qkv_bias[:, head_dim:].reshape(-1))
        .astype(jnp.bfloat16)
        .reshape(FLAG_DEV, heads_dev, 2 * head_dim)
    )
    own_queries = projected[:, :, :head_dim].reshape(row_count, heads_dev * head_dim)
    gathered = lax.all_gather(own_queries, "blk", axis=0, tiled=True)
    prefix_keys = kv_cache[0].at[flagged].set(recomputed[:, :, :head_dim])
    prefix_values = kv_cache[1].at[flagged].set(recomputed[:, :, head_dim:])
    keys_all = jnp.concatenate([prefix_keys, projected[:, :, head_dim : 2 * head_dim]], axis=0)
    values_all = jnp.concatenate([prefix_values, projected[:, :, 2 * head_dim :]], axis=0)
    own_tenant = lax.dynamic_slice_in_dim(row_tenant, own_first, row_count, 0)
    key_tenant = jnp.concatenate([jnp.full((cache_rows,), block_tenant, jnp.int32), own_tenant])
    key_position = jnp.concatenate(
        [jnp.full((cache_rows,), -1, jnp.int32), own_first + jnp.arange(row_count, dtype=jnp.int32)]
    )
    scale = head_dim ** (-0.5)
    qblock = math.gcd(total_rows, 512)
    block_total = total_rows // qblock

    def partial_block(offset):
        query_block = lax.dynamic_slice_in_dim(gathered, offset, qblock, 0).reshape(
            qblock, heads_dev, head_dim
        )
        query_tenant = lax.dynamic_slice_in_dim(row_tenant, offset, qblock, 0)
        query_position = offset + jnp.arange(qblock, dtype=jnp.int32)
        allowed = (query_tenant[:, None] == key_tenant[None, :]) & (
            key_position[None, :] <= query_position[:, None]
        )
        scores = (
            jnp.einsum("qhd,khd->hqk", query_block, keys_all, preferred_element_type=jnp.float32)
            * scale
        )
        gate = allowed[None, :, :]
        row_peak = jnp.max(jnp.where(gate, scores, MASKED), axis=2)
        weights = jnp.where(gate, jnp.exp(scores - row_peak[:, :, None]), 0.0)
        denominator = jnp.sum(weights, axis=2)
        numerator = jnp.einsum(
            "hqk,khd->qhd",
            weights.astype(jnp.bfloat16),
            values_all,
            preferred_element_type=jnp.float32,
        )
        return (numerator.reshape(qblock, heads_dev * head_dim), denominator.T, row_peak.T)

    def fill_block(step_index, buffers):
        numer_buf, denom_buf, peak_buf = buffers
        offset = step_index * qblock
        numerator, denominator, row_peak = partial_block(offset)
        numer_buf = lax.dynamic_update_slice_in_dim(numer_buf, numerator, offset, 0)
        denom_buf = lax.dynamic_update_slice_in_dim(denom_buf, denominator, offset, 0)
        peak_buf = lax.dynamic_update_slice_in_dim(peak_buf, row_peak, offset, 0)
        return (numer_buf, denom_buf, peak_buf)

    initial = (
        jnp.zeros((total_rows, heads_dev * head_dim), jnp.float32),
        jnp.zeros((total_rows, heads_dev), jnp.float32),
        jnp.full((total_rows, heads_dev), MASKED, jnp.float32),
    )
    numer_buf, denom_buf, peak_buf = lax.fori_loop(0, block_total, fill_block, initial)
    numer_view = numer_buf.reshape(blk_total, row_count, heads_dev * head_dim)
    denom_view = denom_buf.reshape(blk_total, row_count, heads_dev)
    peak_view = peak_buf.reshape(blk_total, row_count, heads_dev)
    recv_numer, recv_denom, recv_peak = (
        lax.all_to_all(numer_view, "blk", split_axis=0, concat_axis=0, tiled=True),
        lax.all_to_all(denom_view, "blk", split_axis=0, concat_axis=0, tiled=True),
        lax.all_to_all(peak_view, "blk", split_axis=0, concat_axis=0, tiled=True),
    )
    best = jnp.max(recv_peak, axis=0)
    factor = jnp.exp(recv_peak - best[None])
    summed_denom = jnp.sum(factor * recv_denom, axis=0)
    summed_numer = jnp.sum(
        recv_numer.reshape(blk_total, row_count, heads_dev, head_dim) * factor[:, :, :, None],
        axis=0,
    )
    attended = (summed_numer / summed_denom[:, :, None]).astype(jnp.bfloat16)
    fetched = lax.all_gather(out_weight, "blk", axis=1, tiled=True)
    mixed = jnp.einsum("rhd,hde->re", attended, fetched, preferred_element_type=jnp.float32)
    summed = lax.psum_scatter(
        mixed.astype(jnp.bfloat16), "head", scatter_dimension=1, tiled=True
    ).astype(jnp.float32)
    columns = summed.shape[1]
    bias_part = lax.dynamic_slice_in_dim(out_bias, lax.axis_index("head") * columns, columns, 0)
    return (summed + bias_part).astype(jnp.bfloat16)


def solution(mesh):
    return jax.shard_map(
        body,
        mesh=mesh,
        in_specs=(
            P("blk", None),
            P("blk", None),
            P(None, "blk", "head", None),
            P(),
            P(),
            P("blk", "head", None),
            P("head", None),
            P("head", "blk", None),
            P(),
            P(),
            P(),
            P(),
            P("blk"),
        ),
        out_specs=P("blk", "head"),
        check_vma=False,
    )
```

profile of v0, /device:TPU:8, one launch (start us, length us, event | category | flops | bytes accessed | tf_op | source)
XLA Modules:
  0.0 355.3 jit_solution(12156490804968114255)
XLA Ops:
  6.6 0.7 all-gather.4.cloned.1.call-update
  7.3 0.7 reduce.13
  8.0 0.8 reduce-window.17
  8.8 0.8 reduce-window.18
  9.6 0.7 broadcast_subtract_fusion
  10.3 3.2 sort.17
  13.5 0.6 gather_fusion
  14.3 1.3 fusion.58
  15.6 1.3 fusion.59
  16.9 0.7 concatenate.12
  18.2 1.0 convert_reduce_fusion.1
  19.3 1.1 fusion.39
  20.7 1.0 slice_bitcast_fusion.8
  21.7 78.6 %all-gather.4.cloned.1.call-done = bf16[2048,1,768]{2,0,1:T(8,128)(2,1)} async-done(((bf16[32,1,768]{2,0,1:T(8,128)(2,1)}), bf16[2048,1,768]{2,0,1:T(8,128)(2,1)}) %all-gather.4.cloned.1.call-update) | async-done | bytes 3145744 | tf_op jit(solution)/shard_map/all_gather | solution.py:53
  100.3 2.1 fusion.28
  102.4 0.8 scatter_custom_fusion
  103.2 0.8 scatter_custom_fusion.1
  104.0 2.5 fusion.25
  106.5 48.6 %all-gather = bf16[1536,1,256]{2,0,1:T(8,128)(2,1)S(1)} all-gather(bf16[24,1,256]{2,0,1:T(8,128)(2,1)S(1)} %get-tuple-element.211), channel_id=2, replica_groups=mesh['head'=8,'blk'=64] {'blk'}, dimensions={0}, use_global_device_ids=true | all-gather | bytes 798720 | tf_op jit(solution)/shard_map/all_gather | solution.py:71
  155.0 0.7 pad_maximum_fusion
  155.8 0.6 broadcast_in_dim.64
  157.0 11.8 %while.17 = (s32[]{:T(128)}, f32[1536,256]{1,0:T(8,128)S(1)}, f32[1536,1]{0,1:T(1,128)}, f32[1536,1]{0,1:T(1,128)}, s32[1536]{0:T(1024)}, /*index=5*/s32[280]{0:...) while((s32[]{:T(128)}, f32[1536,256]{1,0:T(8,128)S(1)}, ...), condition=%wide.region_15.16_spmd, body=%wide.region_12.15_spmd.sunk | while | flops 149380608 | bytes 2841571 | solution.py:124
  157.0 0.8 dynamic_slice.29
  157.8 1.0 select_reduce_fusion.2
  158.7 1.4 convolution_dynamic-update-slice_fusion.2
  160.3 0.6 constant_dynamic-update-slice_fusion.3
  161.0 0.8 dynamic_slice.29
  161.7 1.0 select_reduce_fusion.2
  162.7 1.4 convolution_dynamic-update-slice_fusion.2
  164.3 0.6 constant_dynamic-update-slice_fusion.3
  164.9 0.8 dynamic_slice.29
  165.7 1.0 select_reduce_fusion.2
  166.6 1.4 convolution_dynamic-update-slice_fusion.2
  168.2 0.6 constant_dynamic-update-slice_fusion.3
  168.8 0.8 reduce.14
  169.6 0.7 reshape.214
  170.3 10.2 %all-to-all-start.1 = ((f32[64,24,1]{1,2,0:T(1,128)}), f32[64,24,1]{1,2,0:T(1,128)S(1)}, u32[]{:S(2)}, u32[]{:S(2)}) async-start(f32[64,24,1]{1,2,0:T(1,128)} %bitcast.20), calls=%async_computation.1 | async-start | bytes 65536 | tf_op jit(solution)/shard_map/all_to_all | solution.py:131
  180.5 0.7 reduce.15
  181.3 10.2 %all-to-all-done.1 = f32[64,24,1]{1,2,0:T(1,128)S(1)} async-done(((f32[64,24,1]{1,2,0:T(1,128)}), f32[64,24,1]{1,2,0:T(1,128)S(1)}, u32[]{:S(2)}, u32[]{:S(2)}) %all-to-all-start.1) | async-done | bytes 6176 | tf_op jit(solution)/shard_map/all_to_all | solution.py:131
  191.5 19.5 %all_to_all.15 = f32[64,24,1]{1,2,0:T(1,128)S(1)} all-to-all(f32[64,24,1]{1,2,0:T(1,128)S(1)} %bitcast.81), channel_id=1, replica_groups=mesh['head'=8,'blk'=64] {'blk'}, dimensions={0} | all-to-all | bytes 12288 | tf_op jit(solution)/shard_map/all_to_all | solution.py:130
  211.0 12.8 %all-to-all-start = ((f32[64,24,256]{2,1,0:T(8,128)}), f32[64,24,256]{2,1,0:T(8,128)S(1)}, u32[]{:S(2)}, u32[]{:S(2)}) async-start(f32[64,24,256]{2,1,0:T(8,128)} %bitcast.74), calls=%async_computation | async-start | bytes 3145728 | tf_op jit(solution)/shard_map/all_to_all | solution.py:129
  223.9 0.6 copy.24
  224.8 24.0 %all-to-all-done = f32[64,24,256]{2,1,0:T(8,128)S(1)} async-done(((f32[64,24,256]{2,1,0:T(8,128)}), f32[64,24,256]{2,1,0:T(8,128)S(1)}, u32[]{:S(2)}, u32[]{:S(2)}) %all-to-all-start) | async-done | bytes 1572896 | tf_op jit(solution)/shard_map/all_to_all | solution.py:129
  249.1 62.4 %all-gather.6.cloned.1.call-done = bf16[1,256,2048]{2,0,1:T(2,128)(2,1)} async-done(((bf16[1,4,2048]{2,0,1:T(2,128)(2,1)}), bf16[1,256,2048]{2,0,1:T(2,128)(2,1)}) %all-gather.6.cloned.1.call-update) | async-done | bytes 1048592 | tf_op jit(solution)/shard_map/all_gather | solution.py:141
  311.4 2.9 convolution_convert_fusion
  314.3 0.8 dynamic_slice.21
  315.1 32.3 %reduce-scatter.2.cloned.1.call-done = bf16[24,256]{1,0:T(8,128)(2,1)} async-done(((bf16[24,2048]{1,0:T(8,128)(2,1)}), bf16[24,256]{1,0:T(8,128)(2,1)}) %reduce-scatter.2.cloned.1.call-update) | async-done | bytes 12304 | tf_op jit(solution)/shard_map/reduce_scatter | solution.py:143
  347.4 1.3 add_convert_fusion
  (53 shorter events, 3.2 us)
Async XLA Ops:
  6.5 7.0 %copy-start = (bf16[256,2048]{1,0:T(8,128)(2,1)S(1)}, bf16[256,2048]{1,0:T(8,128)(2,1)}, u32[]{:S(2)}) copy-start(bf16[256,2048]{1,0:T(8,128)(2,1)} %param.16) | copy-start | bytes 3145732
  6.5 93.7 %slice-start = ((f32[1,768]{1,0:T(1,128)}), f32[1,512]{1,0:T(1,128)S(1)}, s32[]{:S(2)}) async-start(f32[1,768]{1,0:T(1,128)} %param.21), calls=%async_computation.7 | async-start | bytes 4096 | tf_op jit(solution)/shard_map/slice | solution.py:66
  6.5 93.7 %copy-start.7 = (f32[2048]{0:T(1024)S(1)}, f32[2048]{0:T(1024)}, u32[]{:S(2)}) copy-start(f32[2048]{0:T(1024)} %param.18) | copy-start | bytes 24580
  6.5 93.7 %copy-start.6 = (f32[2048]{0:T(1024)S(1)}, f32[2048]{0:T(1024)}, u32[]{:S(2)}) copy-start(f32[2048]{0:T(1024)} %param.19) | copy-start | bytes 24580
  6.5 93.7 %all-gather.4.cloned.1.call-start = ((), (), s32[]{:S(2)}) async-start(), calls=%async_computation.4 | async-start | bytes 3194880 | tf_op jit(solution)/shard_map/all_gather | solution.py:53
  14.1 89.8 %copy-start.2 = (bf16[24,2048]{1,0:T(8,128)(2,1)S(1)}, bf16[24,2048]{1,0:T(8,128)(2,1)}, u32[]{:S(2)}) copy-start(bf16[24,2048]{1,0:T(8,128)(2,1)} %param.15) | copy-start | bytes 294916
  14.3 6.4 %copy-start.4 = (s32[1536]{0:T(1024)}, s32[1536]{0:T(1024)S(1)}, u32[]{:S(2)}) copy-start(s32[1536]{0:T(1024)S(1)} %convert_reduce_fusion.2) | copy-start | bytes 18436
  157.0 3.1 copy-start.3
  160.9 3.1 copy-start.3
  164.9 3.1 copy-start.3
  168.8 42.1 %copy-start.1 = (f32[1536,256]{1,0:T(8,128)}, f32[1536,256]{1,0:T(8,128)S(1)}, u32[]{:S(2)}) copy-start(f32[1536,256]{1,0:T(8,128)S(1)} %get-tuple-element.178) | copy-start | bytes 4718596
  168.8 55.0 %copy-start.5 = (bf16[1,4,2048]{2,1,0:T(4,128)(2,1)S(1)}, bf16[1,4,2048]{2,1,0:T(4,128)(2,1)}, u32[]{:S(2)}) copy-start(bf16[1,4,2048]{2,1,0:T(4,128)(2,1)} %param.22) | copy-start | bytes 49156
  170.3 21.2 %all-to-all-start.1 = ((f32[64,24,1]{1,2,0:T(1,128)}), f32[64,24,1]{1,2,0:T(1,128)S(1)}, u32[]{:S(2)}, u32[]{:S(2)}) async-start(f32[64,24,1]{1,2,0:T(1,128)} %bitcast.20), calls=%async_computation.1 | async-start | bytes 65536 | tf_op jit(solution)/shard_map/all_to_all | solution.py:131
  211.0 37.8 %all-to-all-start = ((f32[64,24,256]{2,1,0:T(8,128)}), f32[64,24,256]{2,1,0:T(8,128)S(1)}, u32[]{:S(2)}, u32[]{:S(2)}) async-start(f32[64,24,256]{2,1,0:T(8,128)} %bitcast.74), calls=%async_computation | async-start | bytes 3145728 | tf_op jit(solution)/shard_map/all_to_all | solution.py:129
  223.8 87.6 %all-gather.6.cloned.1.call-start = ((), (), s32[]{:S(2)}) async-start(), calls=%async_computation.5 | async-start | bytes 2129920 | tf_op jit(solution)/shard_map/all_gather | solution.py:141
  224.5 122.9 %reduce-scatter.2.cloned.1.call-start = ((), (), s32[]{:S(2)}) async-start(), calls=%async_computation.6 | async-start | bytes 110592 | tf_op jit(solution)/shard_map/reduce_scatter | solution.py:143
Sparse Core Ops, SparseCore 0:
  10.4 89.7 all-gather.3
  227.7 83.7 all-gather.5
  314.5 32.9 reduce-scatter.1
where the time goes:
time: 356 us; the launch traced here: 355 us
  waiting for transfers between devices  208 us (58%)
  blocking collectives  68 us (19%)
  starting transfers between devices  23.1 us (6%)
  other arithmetic  15.8 us (4%)
  matrix products  14.5 us (4%)
  between operations  13.3 us (4%)
  local copies, waits for them, and re-layouts  12.2 us (3%)
    all_gather x1, waiting for transfers between devices, body(): fetched = lax.all_gather(qkv_weight, 'blk', axis=0, tiled=True)  78.6 us
    all_gather x1, waiting for transfers between devices, body(): fetched = lax.all_gather(out_weight, 'blk', axis=1, tiled=True)  62.4 us
    all_gather x1, blocking collectives, body(): gathered = lax.all_gather(own_queries, 'blk', axis=0, tiled=True)  48.6 us
    reduce_scatter x1, waiting for transfers between devices, body(): lax.psum_scatter(mixed.astype(jnp.bfloat16), 'head', scatter_dimension=1,...  32.3 us
    all_to_all x1, waiting for transfers between devices, body(): lax.all_to_all(numer_view, 'blk', split_axis=0, concat_axis=0, tiled=True)  24 us
    all_to_all x1, blocking collectives, body(): lax.all_to_all(denom_view, 'blk', split_axis=0, concat_axis=0, tiled=True)  19.5 us
    all_to_all x1, starting transfers between devices, body(): lax.all_to_all(numer_view, 'blk', split_axis=0, concat_axis=0, tiled=True)  12.8 us
    all_to_all x1, waiting for transfers between devices, body(): lax.all_to_all(peak_view, 'blk', split_axis=0, concat_axis=0, tiled=True)  10.2 us
  transfers between devices with their start and end apart: 5, of which 5 were waited for; matrix products, arithmetic and copies ran while one was open for 5% of the time, Pallas kernels for 0%

commit v1 on v0

--- a/solution.py
+++ b/solution.py
@@ -68,7 +68,19 @@
         .reshape(FLAG_DEV, heads_dev, 2 * head_dim)
     )
     own_queries = projected[:, :, :head_dim].reshape(row_count, heads_dev * head_dim)
-    gathered = lax.all_gather(own_queries, "blk", axis=0, tiled=True)
+
+    def hold_tables(inputs, ax_name, out_dim):
+        degree = lax.axis_size(ax_name)
+        series = []
+        dev = 0
+        while dev < inputs.ndim:
+            series.append(degree if dev == out_dim else 1)
+            dev = dev + 1
+        return lax.all_to_all(
+            jnp.tile(inputs, series), ax_name, split_axis=out_dim, concat_axis=out_dim, tiled=True
+        )
+
+    gathered = hold_tables(own_queries, "blk", 0)
     prefix_keys = kv_cache[0].at[flagged].set(recomputed[:, :, :head_dim])
     prefix_values = kv_cache[1].at[flagged].set(recomputed[:, :, head_dim:])
     keys_all = jnp.concatenate([prefix_keys, projected[:, :, head_dim : 2 * head_dim]], axis=0)

time: 356 us -> 324 us (0.910)
  blocking collectives: 68 us -> 15.7 us
  waiting for transfers between devices: 208 us -> 230 us
    all_gather x1 -> x0, blocking collectives: 48.6 us -> none  [body(): gathered = lax.all_gather(own_queries, 'blk', axis=0, tiled=True)]
    all_to_all x1, waiting for transfers between devices: 24 us -> 35.8 us  [body(): lax.all_to_all(numer_view, 'blk', split_axis=0, concat_axis=0, tiled=True)]
    all_to_all x0 -> x1, waiting for transfers between devices: none -> 11.5 us  [hold_tables(): lax.all_to_all(jnp.tile(inputs, series), ax_name, split_axis=out_dim, con...]
    all_to_all x0 -> x1, starting transfers between devices: none -> 9.24 us  [hold_tables(): lax.all_to_all(jnp.tile(inputs, series), ax_name, split_axis=out_dim, con...]
    all_to_all x1, starting transfers between devices: 12.8 us -> 5.56 us  [body(): lax.all_to_all(numer_view, 'blk', split_axis=0, concat_axis=0, tiled=True)]
    all_gather x1, waiting for transfers between devices: 62.4 us -> 55.5 us  [body(): fetched = lax.all_gather(out_weight, 'blk', axis=1, tiled=True)]
    all_gather x1, waiting for transfers between devices: 78.6 us -> 84 us  [body(): fetched = lax.all_gather(qkv_weight, 'blk', axis=0, tiled=True)]
    all_to_all x1, blocking collectives: 19.5 us -> 15.7 us  [body(): lax.all_to_all(denom_view, 'blk', split_axis=0, concat_axis=0, tiled=True)]
  transfers between devices with their start and end apart: 5 -> 6, of which waited for: 5 -> 6; matrix products, arithmetic and copies ran while one was open for 5% -> 6% of each run, Pallas kernels for 0% -> 0%
where the time goes in v1:
time: 324 us; the launch traced here: 323 us
  waiting for transfers between devices  230 us (71%)
  starting transfers between devices  21.7 us (7%)
  blocking collectives  15.7 us (5%)
  other arithmetic  15.2 us (5%)
  matrix products  14.6 us (5%)
  between operations  13.4 us (4%)
  local copies, waits for them, and re-layouts  12.1 us (4%)
    all_gather x1, waiting for transfers between devices, body(): fetched = lax.all_gather(qkv_weight, 'blk', axis=0, tiled=True)  84 us
    all_gather x1, waiting for transfers between devices, body(): fetched = lax.all_gather(out_weight, 'blk', axis=1, tiled=True)  55.5 us
    all_to_all x1, waiting for transfers between devices, body(): lax.all_to_all(numer_view, 'blk', split_axis=0, concat_axis=0, tiled=True)  35.8 us
    reduce_scatter x1, waiting for transfers between devices, body(): lax.psum_scatter(mixed.astype(jnp.bfloat16), 'head', scatter_dimension=1,...  32.3 us
    all_to_all x1, blocking collectives, body(): lax.all_to_all(denom_view, 'blk', split_axis=0, concat_axis=0, tiled=True)  15.7 us
    all_to_all x1, waiting for transfers between devices, hold_tables(): lax.all_to_all(jnp.tile(inputs, series), ax_name, split_axis=out_dim, con...  11.5 us
    all_to_all x1, waiting for transfers between devices, body(): lax.all_to_all(peak_view, 'blk', split_axis=0, concat_axis=0, tiled=True)  10.2 us
    all_to_all x1, starting transfers between devices, hold_tables(): lax.all_to_all(jnp.tile(inputs, series), ax_name, split_axis=out_dim, con...  9.24 us
  transfers between devices with their start and end apart: 6, of which 6 were waited for; matrix products, arithmetic and copies ran while one was open for 6% of the time, Pallas kernels for 0%

profile of v1, /device:TPU:8, one launch (start us, length us, event | category | flops | bytes accessed | tf_op | source)
XLA Modules:
  0.0 322.9 jit_solution(11943088617724902616)
XLA Ops:
  6.5 0.7 all-gather.3.cloned.1.call-update
  7.3 0.7 broadcast_subtract_fusion
  7.9 3.2 sort.17
  11.1 0.7 reduce.13
  11.8 0.8 reduce-window.17
  12.6 1.3 fusion.58
  14.1 1.0 convert_reduce_fusion.1
  15.1 1.1 fusion.39
  16.2 84.0 %all-gather.3.cloned.1.call-done = bf16[2048,1,768]{2,0,1:T(8,128)(2,1)} async-done(((bf16[32,1,768]{2,0,1:T(8,128)(2,1)}), bf16[2048,1,768]{2,0,1:T(8,128)(2,1)}) %all-gather.3.cloned.1.call-update) | async-done | bytes 3145744 | tf_op jit(solution)/shard_map/all_gather | solution.py:53
  100.2 2.6 fusion.25
  102.9 0.9 tile.9
  103.8 9.2 %all-to-all-start = ((bf16[64,24,256]{2,1,0:T(8,128)(2,1)}), bf16[64,24,256]{2,1,0:T(8,128)(2,1)S(1)}, u32[]{:S(2)}, u32[]{:S(2)}) async-start(bf16[64,24,256]{2,1,0:T(8,128)(2,1)} %tile.9), calls=%async_computation | async-start | bytes 1572864 | tf_op jit(solution)/shard_map/all_to_all | solution.py:79
  113.2 0.6 gather_fusion
  114.0 1.3 fusion.59
  115.3 0.6 concatenate.12
  116.9 2.1 fusion.28
  119.0 0.8 scatter_custom_fusion
  119.8 0.8 scatter_custom_fusion.1
  120.6 0.7 pad_maximum_fusion
  121.3 11.5 %all-to-all-done = bf16[64,24,256]{2,1,0:T(8,128)(2,1)S(1)} async-done(((bf16[64,24,256]{2,1,0:T(8,128)(2,1)}), bf16[64,24,256]{2,1,0:T(8,128)(2,1)S(1)}, u32[]{:S(2)}, u32[]{:S(2)}) %all-to-all-start) | async-done | bytes 786464 | tf_op jit(solution)/shard_map/all_to_all | solution.py:79
  132.9 0.6 broadcast_in_dim.64
  134.1 11.8 %while.17 = (s32[]{:T(128)}, f32[1536,256]{1,0:T(8,128)S(1)}, f32[1536,1]{0,1:T(1,128)}, f32[1536,1]{0,1:T(1,128)}, s32[1536]{0:T(1024)}, /*index=5*/s32[280]{0:...) while((s32[]{:T(128)}, f32[1536,256]{1,0:T(8,128)S(1)}, ...), condition=%wide.region_15.16_spmd, body=%wide.region_12.15_spmd.sunk | while | flops 149380608 | bytes 2841571 | solution.py:136
  134.1 0.8 dynamic_slice.29
  134.8 1.0 select_reduce_fusion.2
  135.8 1.4 convolution_dynamic-update-slice_fusion.2
  137.4 0.6 constant_dynamic-update-slice_fusion.3
  138.0 0.8 dynamic_slice.29
  138.8 1.0 select_reduce_fusion.2
  139.7 1.4 convolution_dynamic-update-slice_fusion.2
  141.3 0.6 constant_dynamic-update-slice_fusion.3
  141.9 0.8 dynamic_slice.29
  142.7 1.0 select_reduce_fusion.2
  143.7 1.4 convolution_dynamic-update-slice_fusion.2
  145.3 0.6 constant_dynamic-update-slice_fusion.3
  145.9 0.8 reduce.14
  146.7 0.7 reshape.217
  147.3 6.8 %all-to-all-start.2 = ((f32[64,24,1]{1,2,0:T(1,128)}), f32[64,24,1]{1,2,0:T(1,128)S(1)}, u32[]{:S(2)}, u32[]{:S(2)}) async-start(f32[64,24,1]{1,2,0:T(1,128)} %bitcast.21), calls=%async_computation.2 | async-start | bytes 65536 | tf_op jit(solution)/shard_map/all_to_all | solution.py:143
  154.2 0.7 reduce.15
  155.0 10.2 %all-to-all-done.2 = f32[64,24,1]{1,2,0:T(1,128)S(1)} async-done(((f32[64,24,1]{1,2,0:T(1,128)}), f32[64,24,1]{1,2,0:T(1,128)S(1)}, u32[]{:S(2)}, u32[]{:S(2)}) %all-to-all-start.2) | async-done | bytes 6176 | tf_op jit(solution)/shard_map/all_to_all | solution.py:143
  165.2 15.7 %all_to_all.24 = f32[64,24,1]{1,2,0:T(1,128)S(1)} all-to-all(f32[64,24,1]{1,2,0:T(1,128)S(1)} %bitcast.83), channel_id=1, replica_groups=mesh['head'=8,'blk'=64] {'blk'}, dimensions={0} | all-to-all | bytes 12288 | tf_op jit(solution)/shard_map/all_to_all | solution.py:142
  181.0 5.6 %all-to-all-start.1 = ((f32[64,24,256]{2,1,0:T(8,128)}), f32[64,24,256]{2,1,0:T(8,128)S(1)}, u32[]{:S(2)}, u32[]{:S(2)}) async-start(f32[64,24,256]{2,1,0:T(8,128)} %bitcast.76), calls=%async_computation.1 | async-start | bytes 3145728 | tf_op jit(solution)/shard_map/all_to_all | solution.py:141
  186.6 0.6 copy.24
  187.5 35.8 %all-to-all-done.1 = f32[64,24,256]{2,1,0:T(8,128)S(1)} async-done(((f32[64,24,256]{2,1,0:T(8,128)}), f32[64,24,256]{2,1,0:T(8,128)S(1)}, u32[]{:S(2)}, u32[]{:S(2)}) %all-to-all-start.1) | async-done | bytes 1572896 | tf_op jit(solution)/shard_map/all_to_all | solution.py:141
  223.6 55.5 %all-gather.5.cloned.1.call-done = bf16[1,256,2048]{2,0,1:T(2,128)(2,1)} async-done(((bf16[1,4,2048]{2,0,1:T(2,128)(2,1)}), bf16[1,256,2048]{2,0,1:T(2,128)(2,1)}) %all-gather.5.cloned.1.call-update) | async-done | bytes 1048592 | tf_op jit(solution)/shard_map/all_gather | solution.py:153
  279.0 2.9 convolution_convert_fusion
  281.9 0.8 dynamic_slice.21
  282.7 32.3 %reduce-scatter.2.cloned.1.call-done = bf16[24,256]{1,0:T(8,128)(2,1)} async-done(((bf16[24,2048]{1,0:T(8,128)(2,1)}), bf16[24,256]{1,0:T(8,128)(2,1)}) %reduce-scatter.2.cloned.1.call-update) | async-done | bytes 12304 | tf_op jit(solution)/shard_map/reduce_scatter | solution.py:155
  315.0 1.3 add_convert_fusion
  (57 shorter events, 3.4 us)
Async XLA Ops:
  6.5 106.7 %copy-start = (bf16[256,2048]{1,0:T(8,128)(2,1)S(1)}, bf16[256,2048]{1,0:T(8,128)(2,1)}, u32[]{:S(2)}) copy-start(bf16[256,2048]{1,0:T(8,128)(2,1)} %param.16) | copy-start | bytes 3145732
  6.5 93.7 %all-gather.3.cloned.1.call-start = ((), (), s32[]{:S(2)}) async-start(), calls=%async_computation.5 | async-start | bytes 3194880 | tf_op jit(solution)/shard_map/all_gather | solution.py:53
  14.1 99.8 %copy-start.4 = (s32[1536]{0:T(1024)}, s32[1536]{0:T(1024)S(1)}, u32[]{:S(2)}) copy-start(s32[1536]{0:T(1024)S(1)} %convert_reduce_fusion.2) | copy-start | bytes 18436
  16.2 96.8 %copy-start.8 = (s32[4]{0:T(128)S(1)}, s32[4]{0:T(128)}, u32[]{:S(2)}) copy-start(s32[4]{0:T(128)} %param.25) | copy-start | bytes 52
  102.8 14.1 %copy-start.2 = (bf16[2,256,1,256]{3,1,2,0:T(8,128)(2,1)S(1)}, bf16[2,256,1,256]{3,1,2,0:T(8,128)(2,1)}, u32[]{:S(2)}) copy-start(bf16[2,256,1,256]{3,1,2,0:T(8,128)(2,1)} %param.17) | copy-start | bytes 786436
  102.8 14.1 %slice-start = ((f32[1,768]{1,0:T(1,128)}), f32[1,512]{1,0:T(1,128)S(1)}, s32[]{:S(2)}) async-start(f32[1,768]{1,0:T(1,128)} %param.21), calls=%async_computation.8 | async-start | bytes 4096 | tf_op jit(solution)/shard_map/slice | solution.py:66
  102.8 14.1 %copy-start.6 = (f32[2048]{0:T(1024)S(1)}, f32[2048]{0:T(1024)}, u32[]{:S(2)}) copy-start(f32[2048]{0:T(1024)} %param.19) | copy-start | bytes 24580
  102.8 14.1 %copy-start.7 = (f32[2048]{0:T(1024)S(1)}, f32[2048]{0:T(1024)}, u32[]{:S(2)}) copy-start(f32[2048]{0:T(1024)} %param.18) | copy-start | bytes 24580
  103.8 29.0 %all-to-all-start = ((bf16[64,24,256]{2,1,0:T(8,128)(2,1)}), bf16[64,24,256]{2,1,0:T(8,128)(2,1)S(1)}, u32[]{:S(2)}, u32[]{:S(2)}) async-start(bf16[64,24,256]{2,1,0:T(8,128)(2,1)} %tile.9), calls=%async_computation | async-start | bytes 1572864 | tf_op jit(solution)/shard_map/all_to_all | solution.py:79
  134.1 3.1 copy-start.3
  138.0 3.1 copy-start.3
  141.9 3.1 copy-start.3
  145.9 35.1 %copy-start.1 = (f32[1536,256]{1,0:T(8,128)}, f32[1536,256]{1,0:T(8,128)S(1)}, u32[]{:S(2)}) copy-start(f32[1536,256]{1,0:T(8,128)S(1)} %get-tuple-element.178) | copy-start | bytes 4718596
  145.9 40.7 %copy-start.5 = (bf16[1,4,2048]{2,1,0:T(4,128)(2,1)S(1)}, bf16[1,4,2048]{2,1,0:T(4,128)(2,1)}, u32[]{:S(2)}) copy-start(bf16[1,4,2048]{2,1,0:T(4,128)(2,1)} %param.22) | copy-start | bytes 49156
  147.3 17.9 %all-to-all-start.2 = ((f32[64,24,1]{1,2,0:T(1,128)}), f32[64,24,1]{1,2,0:T(1,128)S(1)}, u32[]{:S(2)}, u32[]{:S(2)}) async-start(f32[64,24,1]{1,2,0:T(1,128)} %bitcast.21), calls=%async_computation.2 | async-start | bytes 65536 | tf_op jit(solution)/shard_map/all_to_all | solution.py:143
  181.0 42.3 %all-to-all-start.1 = ((f32[64,24,256]{2,1,0:T(8,128)}), f32[64,24,256]{2,1,0:T(8,128)S(1)}, u32[]{:S(2)}, u32[]{:S(2)}) async-start(f32[64,24,256]{2,1,0:T(8,128)} %bitcast.76), calls=%async_computation.1 | async-start | bytes 3145728 | tf_op jit(solution)/shard_map/all_to_all | solution.py:141
  186.5 92.5 %all-gather.5.cloned.1.call-start = ((), (), s32[]{:S(2)}) async-start(), calls=%async_computation.6 | async-start | bytes 2129920 | tf_op jit(solution)/shard_map/all_gather | solution.py:153
  187.3 127.8 %reduce-scatter.2.cloned.1.call-start = ((), (), s32[]{:S(2)}) async-start(), calls=%async_computation.7 | async-start | bytes 110592 | tf_op jit(solution)/shard_map/reduce_scatter | solution.py:155
Sparse Core Ops, SparseCore 0:
  10.4 89.7 all-gather.2
  190.4 88.5 all-gather.4
  282.1 32.9 reduce-scatter.1
